TPU v7x, 32 devices: a whole 2x2x4 slice. The times are simulated.
32 devices in a mesh: groups: 2 (over x), seq: 16 (over z, y, core).
Axes of the slice: x: 2, y: 2, z: 4, core: 2. Of those that a mesh axis runs over, the one named last changes fastest.
Arguments:
- target_queries: bfloat16 [16384, 1024], P(('groups', 'seq')), parts along dimension 0, may hold values from -8 to 8
- memory_keys: bfloat16 [16384, 1024], P(('groups', 'seq')), parts along dimension 0, may hold values from -8 to 8
- memory_values: bfloat16 [16384, 1024], P(('groups', 'seq')), parts along dimension 0, may hold values from -6 to 6
- grad_output: bfloat16 [16384, 1024], P(('groups', 'seq')), parts along dimension 0, may hold values from -6 to 6
- band_start: int32 [128], P(('groups', 'seq')), parts along dimension 0, may hold values from 0 to 63, as said below
- band_end: int32 [128], P(('groups', 'seq')), parts along dimension 0, may hold values from 4 to 64, as said below
Outputs:
- attended: bfloat16 [16384, 1024], P(('groups', 'seq')), parts along dimension 0
- grad_queries: bfloat16 [16384, 1024], P(('groups', 'seq')), parts along dimension 0
- grad_keys: bfloat16 [16384, 1024], P(('groups', 'seq')), parts along dimension 0
- grad_values: bfloat16 [16384, 1024], P(('groups', 'seq')), parts along dimension 0
There are 2 independent parts, one for each index of `groups`. A program takes and returns all parts, laid end to end along the dimension named above; each array names one. Nothing has to cross between parts.
Inputs may be any that keep to these rules, and one draw needn't show every extreme that they name: band_start never falls as the target block b grows, and band_start[b] lies between b - 3 and b. band_end never falls as b grows, and band_end[b] - band_start[b] lies between 1 and 4; the difference 4 occurs in every draw.
All inputs are finite; a program needn't handle non-finite values.
Results may differ from a plain program's by a relative error of at most 0.024.
Values may be sent and summed in bfloat16 or wider, within the bound.
No kernel may reach another device: no remote copies, remote signals or barrier semaphores. Data moves between devices by JAX's collectives and lax.ppermute only.
A program may use at most 128 MiB of HBM per device.

v0:
```python
import math

import jax
import jax.numpy as jnp
from jax import lax
from jax.sharding import PartitionSpec as P

H = 16
BLOCK = 128
MAX_BAND = 4


def padded(cells, sides, width):
    for axis, dim in sides:
        count = lax.axis_size(axis)
        ends = count - 1
        head = lax.slice_in_dim(cells, 0, width, axis=dim)
        tail = lax.slice_in_dim(cells, cells.shape[dim] - width, cells.shape[dim], axis=dim)
        cells = jnp.concatenate(
            [
                lax.ppermute(tail, axis, [(i, (i + 1) % count) for i in range(ends)]),
                cells,
                lax.ppermute(head, axis, [((i + 1) % count, i) for i in range(ends)]),
            ],
            axis=dim,
        )
    return cells


def shifted(shard, axis, by):
    count = lax.axis_size(axis)
    pairs = [(i, i + by) for i in range(count) if 0 <= i + by < count]
    return lax.ppermute(shard, axis, pairs)


def body(target_queries, memory_keys, memory_values, grad_output, band_start, band_end):
    shard_rows, model_width = target_queries.shape
    local_blocks = shard_rows // BLOCK
    span_rows = MAX_BAND * BLOCK
    head_dim = model_width // H
    score_scale = 1.0 / math.sqrt(head_dim)
    rim_rows = local_blocks * BLOCK
    stacked = jnp.stack([memory_keys, memory_values])
    extended = padded(stacked, (("seq", 1),), rim_rows)
    first_block = lax.axis_index("seq") * local_blocks
    offsets = band_start - first_block + local_blocks
    spans = band_end - band_start
    column_block = jnp.arange(span_rows, dtype=jnp.int32) // BLOCK
    query_blocks = target_queries.reshape(local_blocks, BLOCK, model_width)
    grad_blocks = grad_output.reshape(local_blocks, BLOCK, model_width)

    def one_block(running, inputs):
        query_rows, grad_rows, offset, span = inputs
        corner = (jnp.int32(0), offset * BLOCK, jnp.int32(0))
        window = lax.dynamic_slice(extended, corner, (2, span_rows, model_width))
        query_heads = query_rows.reshape(BLOCK, H, head_dim)
        grad_heads = grad_rows.reshape(BLOCK, H, head_dim)
        key_heads = window[0].reshape(span_rows, H, head_dim)
        value_heads = window[1].reshape(span_rows, H, head_dim)
        scores = (
            jnp.einsum("qhd,khd->hqk", query_heads, key_heads, preferred_element_type=jnp.float32)
            * score_scale
        )
        allowed = column_block < span
        scores = jnp.where(allowed[None, None, :], scores, -1e30)
        row_max = jnp.max(scores, axis=-1, keepdims=True)
        weights = jnp.exp(scores - row_max)
        probs = weights / jnp.sum(weights, axis=-1, keepdims=True)
        probs_low = probs.astype(jnp.bfloat16)
        attended = jnp.einsum(
            "hqk,khd->qhd", probs_low, value_heads, preferred_element_type=jnp.float32
        ).astype(jnp.bfloat16)
        row_dot = jnp.einsum(
            "qhd,qhd->hq", grad_heads, attended, preferred_element_type=jnp.float32
        )
        grad_probs = jnp.einsum(
            "qhd,khd->hqk", grad_heads, value_heads, preferred_element_type=jnp.float32
        )
        grad_scores = (probs * (grad_probs - row_dot[:, :, None])).astype(jnp.bfloat16)
        grad_query = (
            jnp.einsum("hqk,khd->qhd", grad_scores, key_heads, preferred_element_type=jnp.float32)
            * score_scale
        ).astype(jnp.bfloat16)
        grad_key = (
            jnp.einsum("hqk,qhd->khd", grad_scores, query_heads, preferred_element_type=jnp.float32)
            * score_scale
        )
        grad_value = jnp.einsum(
            "hqk,qhd->khd", probs_low, grad_heads, preferred_element_type=jnp.float32
        )
        update = jnp.stack(
            [grad_key.reshape(span_rows, model_width), grad_value.reshape(span_rows, model_width)]
        )
        current = lax.dynamic_slice(running, corner, (2, span_rows, model_width))
        running = lax.dynamic_update_slice(running, current + update, corner)
        return (
            running,
            (attended.reshape(BLOCK, model_width), grad_query.reshape(BLOCK, model_width)),
        )

    totals = jnp.zeros((2, shard_rows + 2 * rim_rows, model_width), jnp.float32)
    totals, (attended, grad_query) = lax.scan(
        one_block, totals, (query_blocks, grad_blocks, offsets, spans)
    )
    lower_rim = totals[:, :rim_rows].astype(jnp.bfloat16)
    upper_rim = totals[:, rim_rows + shard_rows :].astype(jnp.bfloat16)
    from_above = shifted(lower_rim, "seq", -1).astype(jnp.float32)
    from_below = shifted(upper_rim, "seq", 1).astype(jnp.float32)
    owned = totals[:, rim_rows : rim_rows + shard_rows]
    owned = owned.at[:, shard_rows - rim_rows :].add(from_above)
    owned = owned.at[:, :rim_rows].add(from_below)
    return (
        attended.reshape(shard_rows, model_width),
        grad_query.reshape(shard_rows, model_width),
        owned[0].astype(jnp.bfloat16),
        owned[1].astype(jnp.bfloat16),
    )


def solution(mesh):
    return jax.shard_map(
        body,
        mesh=mesh,
        in_specs=(
            P(("groups", "seq"), None),
            P(("groups", "seq"), None),
            P(("groups", "seq"), None),
            P(("groups", "seq"), None),
            P(("groups", "seq")),
            P(("groups", "seq")),
        ),
        out_specs=(
            P(("groups", "seq"), None),
            P(("groups", "seq"), None),
            P(("groups", "seq"), None),
            P(("groups", "seq"), None),
        ),
        check_vma=False,
    )
```

profile of v0, /device:TPU:9, one launch (start us, length us, event | category | flops | bytes accessed | tf_op | source)
XLA Modules:
  0.0 298.8 jit_solution(6322734919631548838)
XLA Ops:
  7.8 3.0 %collective-permute-start = (bf16[2,512,1024]{1,2,0:T(8,128)(2,1)}, bf16[2,512,1024]{1,2,0:T(8,128)(2,1)}, u32[]{:S(2)}, u32[]{:S(2)}) collective-permute-start(bf16[2,512,1024]{1,2,0:T(8,128)(2,1)} %pad_maximum_fusion.1), channel_id=1, source_target_pairs={{0,1},{1,2},{2,3},{3,4},{4,5},{5,6},{6,7},{7,8},{8,9},{9,10},{10,1... | collective-permute-start | bytes 6291464 | tf_op jit(solution)/shard_map/ppermute | solution.py:21
  10.9 44.5 %collective-permute-done.1 = bf16[2,512,1024]{1,2,0:T(8,128)(2,1)} collective-permute-done((bf16[2,512,1024]{1,2,0:T(8,128)(2,1)}, bf16[2,512,1024]{1,2,0:T(8,128)(2,1)}, u32[]{:S(2)}, u32[]{:S(2)}) %collective-permute-start.1) | collective-permute-done | bytes 2097184 | tf_op jit(solution)/shard_map/ppermute | solution.py:23
  55.5 5.4 %pad_maximum_fusion = bf16[2,1536,1024]{1,2,0:T(8,128)(2,1)} fusion(bf16[2,512,1024]{1,2,0:T(8,128)(2,1)} %collective-permute-done.1, bf16[1,512,1024]{1,2,0:T(8,128)(2,1)S(1)} %bitcast.111, bf16[1,512,1024]{1,2,0:T(8,128)(2,1)S(1)} %bitcast.109, bf16[2,512,1024]{1,2,0:T(8,128)(2,1)} %collective-permute-done), kind=kLoop, calls=%fused_computation.37 | loop fusion | flops 25165824 | bytes 12582912 | tf_op jit(solution)/shard_map/concatenate | solution.py:19
  60.9 6.1 %broadcast_in_dim.26.clone = f32[2,1536,1024]{2,1,0:T(8,128)} broadcast(f32[]{:T(128)} %constant.115.clone.1), dimensions={} | broadcast | bytes 12582916 | tf_op jit(solution)/shard_map/broadcast_in_dim | solution.py:101
  67.1 170.1 %while.19 = (s32[]{:T(128)}, f32[2,1536,1024]{2,1,0:T(8,128)}, bf16[4,128,1024]{2,1,0:T(8,128)(2,1)}, bf16[4,128,1024]{2,1,0:T(8,128)(2,1)}, s32[4]{0:T(128)S(1)...) while((s32[]{:T(128)}, f32[2,1536,1024]{2,1,0:T(8,128)}, ...), condition=%wide.region_3.4_spmd.clone, body=%wide.region_0.3_spmd.clone.sunk | while | flops 819334144 | bytes 123512120 | solution.py:102
  73.6 4.8 %constant_dynamic-slice_fusion.9 = f32[2,512,1024]{2,1,0:T(8,128)} fusion(f32[2,1536,1024]{2,1,0:T(8,128)} %get-tuple-element.248, s32[]{:T(128)S(6)} %select_n.39), kind=kLoop, calls=%fused_computation.33.clone.1 | loop fusion | bytes 8388612 | tf_op jit(solution)/shard_map/while/body/eval_jaxpr/dynamic_slice | solution.py:94
  78.4 5.4 %copy.46 = f32[2,512,1024]{1,2,0:T(8,128)} copy(f32[2,512,1024]{2,1,0:T(8,128)} %constant_dynamic-slice_fusion.9) | data formatting | bytes 8388608 | tf_op jit(solution)/shard_map/while/body/eval_jaxpr/dynamic_slice | solution.py:94
  83.7 3.5 %fusion.67 = (f32[16,128]{1,0:T(8,128)S(1)}, f32[16,128,512]{2,1,0:T(8,128)}) fusion(pred[512]{0:T(512)(128)(4,1)S(1)} %fusion.66, bf16[128,16,64]{0,2,1:T(8,128)(2,1)S(1)} %bitcast.105, bf16[512,16,64]{0,2,1:T(8,128)(2,1)S(1)} %bitcast.99), kind=kOutput, calls=%fused_computation.43.clone.1 | convolution fusion | flops 138412544 | bytes 5513728 | tf_op jit(solution)/shard_map/while/body/eval_jaxpr/sub | solution.py:67
  95.2 3.0 %maximum_add_fusion.2 = f32[2,512,1024]{1,2,0:T(8,128)} fusion(f32[2,512,1024]{1,2,0:T(8,128)S(1)} %copy-done, f32[1,512,1024]{1,2,0:T(8,128)S(1)} %bitcast.95, f32[1,512,1024]{1,2,0:T(8,128)S(1)} %bitcast.96), kind=kLoop, calls=%fused_computation.2.clone.1 | loop fusion | flops 2097152 | bytes 12582912 | tf_op jit(solution)/shard_map/while/body/eval_jaxpr/add | solution.py:95
  98.2 5.4 %copy.49 = f32[2,512,1024]{2,1,0:T(8,128)} copy(f32[2,512,1024]{1,2,0:T(8,128)} %maximum_add_fusion.2) | data formatting | bytes 8388608 | tf_op jit(solution)/shard_map/while/body/eval_jaxpr/dynamic_update_slice | solution.py:95
  104.7 4.8 %constant_dynamic-update-slice_fusion.5 = f32[2,1536,1024]{2,1,0:T(8,128)} fusion(f32[2,1536,1024]{2,1,0:T(8,128)} %get-tuple-element.248, f32[2,512,1024]{2,1,0:T(8,128)} %copy.49, s32[]{:T(128)S(6)} %select_n.39), kind=kLoop, calls=%fused_computation.29.clone.1 | loop fusion | bytes 8388612 | tf_op jit(solution)/shard_map/while/body/eval_jaxpr/dynamic_update_slice | solution.py:95
  116.0 4.8 %constant_dynamic-slice_fusion.9 = f32[2,512,1024]{2,1,0:T(8,128)} fusion(f32[2,1536,1024]{2,1,0:T(8,128)} %get-tuple-element.248, s32[]{:T(128)S(6)} %select_n.39), kind=kLoop, calls=%fused_computation.33.clone.1 | loop fusion | bytes 8388612 | tf_op jit(solution)/shard_map/while/body/eval_jaxpr/dynamic_slice | solution.py:94
  120.8 5.4 %copy.46 = f32[2,512,1024]{1,2,0:T(8,128)} copy(f32[2,512,1024]{2,1,0:T(8,128)} %constant_dynamic-slice_fusion.9) | data formatting | bytes 8388608 | tf_op jit(solution)/shard_map/while/body/eval_jaxpr/dynamic_slice | solution.py:94
  126.2 3.5 %fusion.67 = (f32[16,128]{1,0:T(8,128)S(1)}, f32[16,128,512]{2,1,0:T(8,128)}) fusion(pred[512]{0:T(512)(128)(4,1)S(1)} %fusion.66, bf16[128,16,64]{0,2,1:T(8,128)(2,1)S(1)} %bitcast.105, bf16[512,16,64]{0,2,1:T(8,128)(2,1)S(1)} %bitcast.99), kind=kOutput, calls=%fused_computation.43.clone.1 | convolution fusion | flops 138412544 | bytes 5513728 | tf_op jit(solution)/shard_map/while/body/eval_jaxpr/sub | solution.py:67
  140.6 5.4 %copy.49 = f32[2,512,1024]{2,1,0:T(8,128)} copy(f32[2,512,1024]{1,2,0:T(8,128)} %maximum_add_fusion.2) | data formatting | bytes 8388608 | tf_op jit(solution)/shard_map/while/body/eval_jaxpr/dynamic_update_slice | solution.py:95
  147.2 4.9 %constant_dynamic-update-slice_fusion.5 = f32[2,1536,1024]{2,1,0:T(8,128)} fusion(f32[2,1536,1024]{2,1,0:T(8,128)} %get-tuple-element.248, f32[2,512,1024]{2,1,0:T(8,128)} %copy.49, s32[]{:T(128)S(6)} %select_n.39), kind=kLoop, calls=%fused_computation.29.clone.1 | loop fusion | bytes 8388612 | tf_op jit(solution)/shard_map/while/body/eval_jaxpr/dynamic_update_slice | solution.py:95
  158.6 4.8 %constant_dynamic-slice_fusion.9 = f32[2,512,1024]{2,1,0:T(8,128)} fusion(f32[2,1536,1024]{2,1,0:T(8,128)} %get-tuple-element.248, s32[]{:T(128)S(6)} %select_n.39), kind=kLoop, calls=%fused_computation.33.clone.1 | loop fusion | bytes 8388612 | tf_op jit(solution)/shard_map/while/body/eval_jaxpr/dynamic_slice | solution.py:94
  163.4 5.4 %copy.46 = f32[2,512,1024]{1,2,0:T(8,128)} copy(f32[2,512,1024]{2,1,0:T(8,128)} %constant_dynamic-slice_fusion.9) | data formatting | bytes 8388608 | tf_op jit(solution)/shard_map/while/body/eval_jaxpr/dynamic_slice | solution.py:94
  168.7 3.5 %fusion.67 = (f32[16,128]{1,0:T(8,128)S(1)}, f32[16,128,512]{2,1,0:T(8,128)}) fusion(pred[512]{0:T(512)(128)(4,1)S(1)} %fusion.66, bf16[128,16,64]{0,2,1:T(8,128)(2,1)S(1)} %bitcast.105, bf16[512,16,64]{0,2,1:T(8,128)(2,1)S(1)} %bitcast.99), kind=kOutput, calls=%fused_computation.43.clone.1 | convolution fusion | flops 138412544 | bytes 5513728 | tf_op jit(solution)/shard_map/while/body/eval_jaxpr/sub | solution.py:67
  180.2 3.0 %maximum_add_fusion.2 = f32[2,512,1024]{1,2,0:T(8,128)} fusion(f32[2,512,1024]{1,2,0:T(8,128)S(1)} %copy-done, f32[1,512,1024]{1,2,0:T(8,128)S(1)} %bitcast.95, f32[1,512,1024]{1,2,0:T(8,128)S(1)} %bitcast.96), kind=kLoop, calls=%fused_computation.2.clone.1 | loop fusion | flops 2097152 | bytes 12582912 | tf_op jit(solution)/shard_map/while/body/eval_jaxpr/add | solution.py:95
  183.2 5.4 %copy.49 = f32[2,512,1024]{2,1,0:T(8,128)} copy(f32[2,512,1024]{1,2,0:T(8,128)} %maximum_add_fusion.2) | data formatting | bytes 8388608 | tf_op jit(solution)/shard_map/while/body/eval_jaxpr/dynamic_update_slice | solution.py:95
  189.7 4.9 %constant_dynamic-update-slice_fusion.5 = f32[2,1536,1024]{2,1,0:T(8,128)} fusion(f32[2,1536,1024]{2,1,0:T(8,128)} %get-tuple-element.248, f32[2,512,1024]{2,1,0:T(8,128)} %copy.49, s32[]{:T(128)S(6)} %select_n.39), kind=kLoop, calls=%fused_computation.29.clone.1 | loop fusion | bytes 8388612 | tf_op jit(solution)/shard_map/while/body/eval_jaxpr/dynamic_update_slice | solution.py:95
  201.1 4.8 %constant_dynamic-slice_fusion.9 = f32[2,512,1024]{2,1,0:T(8,128)} fusion(f32[2,1536,1024]{2,1,0:T(8,128)} %get-tuple-element.248, s32[]{:T(128)S(6)} %select_n.39), kind=kLoop, calls=%fused_computation.33.clone.1 | loop fusion | bytes 8388612 | tf_op jit(solution)/shard_map/while/body/eval_jaxpr/dynamic_slice | solution.py:94
  205.9 5.4 %copy.46 = f32[2,512,1024]{1,2,0:T(8,128)} copy(f32[2,512,1024]{2,1,0:T(8,128)} %constant_dynamic-slice_fusion.9) | data formatting | bytes 8388608 | tf_op jit(solution)/shard_map/while/body/eval_jaxpr/dynamic_slice | solution.py:94
  211.3 3.5 %fusion.67 = (f32[16,128]{1,0:T(8,128)S(1)}, f32[16,128,512]{2,1,0:T(8,128)}) fusion(pred[512]{0:T(512)(128)(4,1)S(1)} %fusion.66, bf16[128,16,64]{0,2,1:T(8,128)(2,1)S(1)} %bitcast.105, bf16[512,16,64]{0,2,1:T(8,128)(2,1)S(1)} %bitcast.99), kind=kOutput, calls=%fused_computation.43.clone.1 | convolution fusion | flops 138412544 | bytes 5513728 | tf_op jit(solution)/shard_map/while/body/eval_jaxpr/sub | solution.py:67
  222.7 3.0 %maximum_add_fusion.2 = f32[2,512,1024]{1,2,0:T(8,128)} fusion(f32[2,512,1024]{1,2,0:T(8,128)S(1)} %copy-done, f32[1,512,1024]{1,2,0:T(8,128)S(1)} %bitcast.95, f32[1,512,1024]{1,2,0:T(8,128)S(1)} %bitcast.96), kind=kLoop, calls=%fused_computation.2.clone.1 | loop fusion | flops 2097152 | bytes 12582912 | tf_op jit(solution)/shard_map/while/body/eval_jaxpr/add | solution.py:95
  225.7 5.4 %copy.49 = f32[2,512,1024]{2,1,0:T(8,128)} copy(f32[2,512,1024]{1,2,0:T(8,128)} %maximum_add_fusion.2) | data formatting | bytes 8388608 | tf_op jit(solution)/shard_map/while/body/eval_jaxpr/dynamic_update_slice | solution.py:95
  232.3 4.9 %constant_dynamic-update-slice_fusion.5 = f32[2,1536,1024]{2,1,0:T(8,128)} fusion(f32[2,1536,1024]{2,1,0:T(8,128)} %get-tuple-element.248, f32[2,512,1024]{2,1,0:T(8,128)} %copy.49, s32[]{:T(128)S(6)} %select_n.39), kind=kLoop, calls=%fused_computation.29.clone.1 | loop fusion | bytes 8388612 | tf_op jit(solution)/shard_map/while/body/eval_jaxpr/dynamic_update_slice | solution.py:95
  237.2 5.6 %convert.8 = bf16[2,1536,1024]{2,1,0:T(8,128)(2,1)S(1)} convert(f32[2,1536,1024]{2,1,0:T(8,128)} %get-tuple-element.100) | non-fusion elementwise | flops 3145728 | bytes 18874368 | tf_op jit(solution)/shard_map/convert.3
  245.2 4.4 %collective-permute-start.3 = (bf16[2,512,1024]{2,1,0:T(8,128)(2,1)S(1)}, bf16[2,512,1024]{2,1,0:T(8,128)(2,1)S(1)}, u32[]{:S(2)}, u32[]{:S(2)}) collective-permute-start(bf16[2,512,1024]{2,1,0:T(8,128)(2,1)S(1)} %get-tuple-element.157), channel_id=1, source_target_pairs={{0,1},{1,2},{2,3},{3,4},{4,5},{5,6},{6,7},{7,8},{8,9},{9,10},{10,1... | collective-permute-start | bytes 6291464 | tf_op jit(solution)/shard_map/ppermute | solution.py:33
  249.6 44.2 %collective-permute-done.2 = bf16[2,512,1024]{2,1,0:T(8,128)(2,1)S(1)} collective-permute-done((bf16[2,512,1024]{2,1,0:T(8,128)(2,1)S(1)}, bf16[2,512,1024]{2,1,0:T(8,128)(2,1)S(1)}, u32[]{:S(2)}, u32[]{:S(2)}) %collective-permute-start.2) | collective-permute-done | bytes 2097184 | tf_op jit(solution)/shard_map/ppermute | solution.py:33
  293.8 3.5 %add_convert_fusion = bf16[2,512,1024]{2,1,0:T(8,128)(2,1)S(1)} fusion(bf16[2,512,1024]{2,1,0:T(8,128)(2,1)S(1)} %collective-permute-done.3, bf16[2,512,1024]{2,1,0:T(8,128)(2,1)S(1)} %collective-permute-done.2, f32[2,1536,1024]{2,1,0:T(8,128)} %get-tuple-element.100), kind=kLoop, calls=%fused_computation.38 | loop fusion | flops 5242880 | bytes 10485760 | tf_op jit(solution)/shard_map/convert.1
  (101 shorter events, 73.5 us)
Async XLA Ops:
  0.6 10.2 %copy-start.2 = (s32[4]{0:T(128)S(1)}, s32[4]{0:T(128)}, u32[]{:S(2)}) copy-start(s32[4]{0:T(128)} %param.21) | copy-start | bytes 52
  0.6 10.2 %copy-start.3 = (s32[4]{0:T(128)S(1)}, s32[4]{0:T(128)}, u32[]{:S(2)}) copy-start(s32[4]{0:T(128)} %param.20) | copy-start | bytes 52
  5.2 50.2 %collective-permute-start.1 = (bf16[2,512,1024]{1,2,0:T(8,128)(2,1)}, bf16[2,512,1024]{1,2,0:T(8,128)(2,1)}, u32[]{:S(2)}, u32[]{:S(2)}) collective-permute-start(bf16[2,512,1024]{1,2,0:T(8,128)(2,1)} %pad_maximum_fusion.1), channel_id=1, source_target_pairs={{1,0},{2,1},{3,2},{4,3},{5,4},{6,5},{7,6},{8,7},{9,8},{10,9},{11,1... | collective-permute-start | bytes 6291464 | tf_op jit(solution)/shard_map/ppermute | solution.py:23
  7.8 47.8 %collective-permute-start = (bf16[2,512,1024]{1,2,0:T(8,128)(2,1)}, bf16[2,512,1024]{1,2,0:T(8,128)(2,1)}, u32[]{:S(2)}, u32[]{:S(2)}) collective-permute-start(bf16[2,512,1024]{1,2,0:T(8,128)(2,1)} %pad_maximum_fusion.1), channel_id=1, source_target_pairs={{0,1},{1,2},{2,3},{3,4},{4,5},{5,6},{6,7},{7,8},{8,9},{9,10},{10,1... | collective-permute-start | bytes 6291464 | tf_op jit(solution)/shard_map/ppermute | solution.py:21
  89.7 2.2 copy-start.1
  93.0 2.2 copy-start
  132.2 2.2 copy-start.1
  135.4 2.2 copy-start
  174.7 2.2 copy-start.1
  178.0 2.2 copy-start
  217.3 2.2 copy-start.1
  220.5 2.2 copy-start
  243.2 50.6 %collective-permute-start.2 = (bf16[2,512,1024]{2,1,0:T(8,128)(2,1)S(1)}, bf16[2,512,1024]{2,1,0:T(8,128)(2,1)S(1)}, u32[]{:S(2)}, u32[]{:S(2)}) collective-permute-start(bf16[2,512,1024]{2,1,0:T(8,128)(2,1)S(1)} %get-tuple-element.156), channel_id=1, source_target_pairs={{1,0},{2,1},{3,2},{4,3},{5,4},{6,5},{7,6},{8,7},{9,8},{10,9},{11,1... | collective-permute-start | bytes 6291464 | tf_op jit(solution)/shard_map/ppermute | solution.py:33
  245.2 48.6 %collective-permute-start.3 = (bf16[2,512,1024]{2,1,0:T(8,128)(2,1)S(1)}, bf16[2,512,1024]{2,1,0:T(8,128)(2,1)S(1)}, u32[]{:S(2)}, u32[]{:S(2)}) collective-permute-start(bf16[2,512,1024]{2,1,0:T(8,128)(2,1)S(1)} %get-tuple-element.157), channel_id=1, source_target_pairs={{0,1},{1,2},{2,3},{3,4},{4,5},{5,6},{6,7},{7,8},{8,9},{9,10},{10,1... | collective-permute-start | bytes 6291464 | tf_op jit(solution)/shard_map/ppermute | solution.py:33
where the time goes:
time: 301 us; the launch traced here: 299 us
  local copies, waits for them, and re-layouts  125 us (42%)
  waiting for transfers between devices  88.9 us (30%)
  other arithmetic  40.9 us (14%)
  matrix products  28.2 us (9%)
  starting transfers between devices  11.9 us (4%)
  loops' own time  3.04 us (1%)
    ppermute x1, waiting for transfers between devices, padded(): lax.ppermute(head, axis, [((i + 1) % count, i) for i in range(ends)])  44.5 us
    ppermute x2, waiting for transfers between devices, shifted(): return lax.ppermute(shard, axis, pairs)  44.2 us
    dynamic_update_slice x8, local copies, waits for them, and re-layouts, one_block(): running = lax.dynamic_update_slice(running, current + update, corner)  41.1 us
    dynamic_slice x8, local copies, waits for them, and re-layouts, one_block(): current = lax.dynamic_slice(running, corner, (2, span_rows, model_width))  40.6 us
    dynamic_slice x24, local copies, waits for them, and re-layouts, body(): lax.scan(one_block, totals, (query_blocks, grad_blocks, offsets, spans))  13.8 us
    sub x4, matrix products, one_block(): weights = jnp.exp(scores - row_max)  13.8 us
    add x4, other arithmetic, one_block(): running = lax.dynamic_update_slice(running, current + update, corner)  12.1 us
    convert_element_type x4, other arithmetic, one_block(): probs_low = probs.astype(jnp.bfloat16)  10.2 us
  transfers between devices with their start and end apart: 4, of which 3 were waited for; matrix products, arithmetic and copies ran while one was open for 0% of the time, Pallas kernels for 0%

commit v1 on v0

v1 whole, which is shorter than its diff:
```python
import functools
import math

import jax
import jax.numpy as jnp
from jax import lax
from jax.experimental import pallas as pl
from jax.experimental.pallas import tpu as pltpu
from jax.sharding import PartitionSpec as P

H = 16
BLOCK = 128
MAX_BAND = 4
REACH = MAX_BAND - 1
SLOTS = 2
HEADER = 16
PIECES = 2
VMEM_LIMIT = 48 * 1024 * 1024

ANY = pl.BlockSpec(memory_space=pl.ANY)
SMEM = pl.BlockSpec(memory_space=pltpu.SMEM)


def rows(block, count=1):
    if isinstance(block, int):
        return pl.ds(block * BLOCK, count * BLOCK)
    return pl.ds(pl.multiple_of(block * BLOCK, BLOCK), count * BLOCK)


def run_copies(copies):
    for copy in copies:
        copy.start()
    for copy in copies:
        copy.wait()


def moved_up(starts, ends, first, blocks):
    return ends[blocks - 1] == first + blocks + REACH


def moved_down(starts, ends, first):
    return starts[0] == first - REACH


def pack_kernel(blocks, piece, width, header, starts, ends, place, q, k, v, g, inter, intra, head, sem):
    first, odd = place[0], place[1]
    up = moved_up(starts, ends, first, blocks)
    down = moved_down(starts, ends, first)
    cols = pl.ds(piece * width, width)

    def send(message, edge, behind, moves, value, slot):
        def copy(source, block, index):
            return pltpu.make_async_copy(
                source.at[rows(block), cols], message.at[rows(index)], sem.at[slot * 5 + index]
            )

        near = [copy(k, edge, 0), copy(v, edge, 1)]
        target = [copy(q, edge, 2), copy(g, edge, 3)]
        far = [copy(k, behind, 2), copy(v, behind, 3)]
        for c in near:
            c.start()

        @pl.when(moves)
        def _():
            for c in target:
                c.start()

        @pl.when(jnp.logical_not(moves))
        def _():
            for c in far:
                c.start()

        waits = near + far
        if header:
            head[slot] = jnp.full((HEADER, width), value.astype(jnp.float32)).astype(head.dtype)
            tail = pltpu.make_async_copy(
                head.at[slot], message.at[pl.ds(2 * SLOTS * BLOCK, HEADER)], sem.at[slot * 5 + 4]
            )
            tail.start()
            waits = waits + [tail]
        return waits

    up_value = jnp.where(up, MAX_BAND, 0)
    down_value = jnp.where(down, ends[0] - starts[0], 0)
    is_odd = odd == 1
    edge = jnp.where(is_odd, blocks - 1, 0)
    behind = jnp.where(is_odd, blocks - 2, 1)
    moves = jnp.where(is_odd, up.astype(jnp.int32), down.astype(jnp.int32)) == 1
    value = jnp.where(is_odd, up_value, down_value)
    waits = send(inter, edge, behind, moves, value, 0)
    edge = jnp.where(is_odd, 0, blocks - 1)
    behind = jnp.where(is_odd, 1, blocks - 2)
    moves = jnp.where(is_odd, down.astype(jnp.int32), up.astype(jnp.int32)) == 1
    value = jnp.where(is_odd, down_value, up_value)
    waits += send(intra, edge, behind, moves, value, 1)
    for c in waits:
        c.wait()


def pack(blocks, piece, width, starts, ends, place, q, k, v, g):
    header = piece == 0
    shape = jax.ShapeDtypeStruct((2 * SLOTS * BLOCK + (HEADER if header else 0), width), q.dtype)
    return pl.pallas_call(
        functools.partial(pack_kernel, blocks, piece, width, header),
        out_shape=(shape, shape),
        in_specs=[SMEM] * 3 + [ANY] * 4,
        out_specs=(ANY, ANY),
        scratch_shapes=[
            pltpu.VMEM((2, HEADER, width), q.dtype),
            pltpu.SemaphoreType.DMA((10,)),
        ],
        name=f"pack{piece}",
    )(starts, ends, place, q, k, v, g)


def attend_pair(count, head_dim, q_row, k_row, lane, kb, vb, qb, gb, dk, dv, ob, dqb):
    dtype = kb.dtype
    lanes = pl.ds(lane, 2 * head_dim)
    window = pl.ds(k_row, count * BLOCK)
    left = lax.broadcasted_iota(jnp.int32, (BLOCK, 2 * head_dim), 1) < head_dim
    zero = jnp.zeros((BLOCK, 2 * head_dim), dtype)
    q = qb[pl.ds(q_row, BLOCK), lanes] * jnp.asarray(1.0 / math.sqrt(head_dim), dtype)
    g = gb[pl.ds(q_row, BLOCK), lanes]
    q = jnp.concatenate([jnp.where(left, q, zero), jnp.where(left, zero, q)], axis=0)
    g = jnp.concatenate([jnp.where(left, g, zero), jnp.where(left, zero, g)], axis=0)
    keys = kb[window, lanes]
    values = vb[window, lanes]
    by_row = (((1,), (1,)), ((), ()))
    by_key = (((0,), (0,)), ((), ()))
    plain = (((1,), (0,)), ((), ()))
    dot = functools.partial(lax.dot_general, preferred_element_type=jnp.float32)
    scores = dot(keys, q, by_row)
    top = jnp.max(scores, axis=0, keepdims=True)
    weights = jnp.exp(scores - top)
    grad_probs = dot(values, g, by_row)
    scale = 1.0 / jnp.sum(weights, axis=0, keepdims=True)
    row_dot = jnp.sum(weights * grad_probs, axis=0, keepdims=True) * scale
    probs = weights * scale
    low = probs.astype(dtype)
    grad_scores = (probs * (grad_probs - row_dot)).astype(dtype)
    dv[window, lanes] += dot(low, g, plain)
    dk[window, lanes] += dot(grad_scores, q, plain)
    out = dot(values, low, by_key)
    grad_q = dot(keys, grad_scores, by_key) * (1.0 / math.sqrt(head_dim))

    def diagonal(x):
        return jnp.concatenate([x[:head_dim, :BLOCK], x[head_dim:, BLOCK:]], axis=0).T.astype(dtype)

    ob[pl.ds(q_row, BLOCK), lanes] = diagonal(out)
    dqb[pl.ds(q_row, BLOCK), lanes] = diagonal(grad_q)


def attend_kernel(
    blocks, piece, width, head_dim,
    starts, ends, place, q, k, v, g, inter, intra, inter_head, intra_head, *rest
):
    if piece:
        rest = rest[2:]
    attended, grad_q, back_inter, back_intra, grad_k, grad_v = rest[:6]
    kb, vb, qb, gb, dk, dv, ob, dqb, low, head, sem = rest[6:]
    first, odd = place[0], place[1]
    cols = pl.ds(piece * width, width)
    own = rows(SLOTS, blocks)
    count = [0]

    def copy(source, target):
        count[0] += 1
        return pltpu.make_async_copy(source, target, sem.at[count[0] - 1])

    heads = [
        copy(inter_head.at[pl.ds(2 * SLOTS * BLOCK, HEADER)], head.at[0]),
        copy(intra_head.at[pl.ds(2 * SLOTS * BLOCK, HEADER)], head.at[1]),
    ]
    loads = [
        copy(k.at[:, cols], kb.at[own]),
        copy(v.at[:, cols], vb.at[own]),
        copy(q.at[:, cols], qb.at[rows(1, blocks)]),
        copy(g.at[:, cols], gb.at[rows(1, blocks)]),
    ]
    for c in heads + loads:
        c.start()
    is_odd = odd == 1
    for c in heads:
        c.wait()
    from_inter = jnp.max(head[0].astype(jnp.float32)).astype(jnp.int32)
    from_intra = jnp.max(head[1].astype(jnp.float32)).astype(jnp.int32)
    below_span = jnp.where(is_odd, from_intra, from_inter)
    above_span = jnp.where(is_odd, from_inter, from_intra)

    near_below, far_below = SLOTS - 1, SLOTS - 2
    near_above, far_above = SLOTS + blocks, SLOTS + blocks + 1
    base = count[0]

    def arrive(message, near, far, target, span, slot):
        at = lambda i: sem.at[base + slot * 4 + i]
        part = lambda i: message.at[rows(i)]
        make = pltpu.make_async_copy
        always = [make(part(0), kb.at[rows(near)], at(0)), make(part(1), vb.at[rows(near)], at(1))]
        moved = [make(part(2), qb.at[rows(target)], at(2)), make(part(3), gb.at[rows(target)], at(3))]
        stays = [make(part(2), kb.at[rows(far)], at(2)), make(part(3), vb.at[rows(far)], at(3))]
        for c in always:
            c.start()

        @pl.when(span > 0)
        def _():
            for c in moved:
                c.start()

        @pl.when(span == 0)
        def _():
            for c in stays:
                c.start()

        return always + stays

    inter_near = jnp.where(is_odd, near_above, near_below)
    inter_far = jnp.where(is_odd, far_above, far_below)
    inter_target = jnp.where(is_odd, blocks + 1, 0)
    intra_near = jnp.where(is_odd, near_below, near_above)
    intra_far = jnp.where(is_odd, far_below, far_above)
    intra_target = jnp.where(is_odd, 0, blocks + 1)
    loads += arrive(inter, inter_near, inter_far, inter_target, from_inter, 0)
    loads += arrive(intra, intra_near, intra_far, intra_target, from_intra, 1)
    dk[...] = jnp.zeros_like(dk)
    dv[...] = jnp.zeros_like(dv)
    for c in loads:
        c.wait()

    up = moved_up(starts, ends, first, blocks)
    down = moved_down(starts, ends, first)

    def task(index, carry):
        mine = jnp.clip(index - 1, 0, blocks - 1)
        lower, upper = index == 0, index == blocks + 1
        span = ends[mine] - starts[mine]
        gone = ((index == 1) & down) | ((index == blocks) & up)
        span = jnp.where(gone, 0, span)
        span = jnp.where(lower, below_span, jnp.where(upper, above_span, span))
        window = starts[mine] - first + SLOTS
        window = jnp.where(lower, near_below, jnp.where(upper, near_above - REACH, window))
        q_row = pl.multiple_of(index * BLOCK, BLOCK)
        k_row = pl.multiple_of(window * BLOCK, BLOCK)
        for size in range(1, MAX_BAND + 1):

            @pl.when(span == size)
            def _():
                @pl.loop(0, width // (2 * head_dim))
                def _(pair):
                    lane = pl.multiple_of(pair * 2 * head_dim, 2 * head_dim)
                    attend_pair(size, head_dim, q_row, k_row, lane, kb, vb, qb, gb, dk, dv, ob, dqb)

        return carry

    lax.fori_loop(0, blocks + 2, task, 0)

    stores = [
        (ob.at[rows(1, blocks)], attended.at[:, cols]),
        (dqb.at[rows(1, blocks)], grad_q.at[:, cols]),
        (dk.at[own], grad_k),
        (dv.at[own], grad_v),
    ]
    stores = [pltpu.make_async_copy(a, b, sem.at[i]) for i, (a, b) in enumerate(stores)]
    for c in stores:
        c.start()

    def leave(message, near, far, target, span, slot):
        at = lambda i: sem.at[base + slot * 2 + i]
        low[slot, rows(0)] = dk[rows(near)].astype(low.dtype)
        low[slot, rows(1)] = dv[rows(near)].astype(low.dtype)

        @pl.when(span > 0)
        def _():
            low[slot, rows(2)] = ob[rows(target)]
            low[slot, rows(3)] = dqb[rows(target)]

        @pl.when(span == 0)
        def _():
            low[slot, rows(2)] = dk[rows(far)].astype(low.dtype)
            low[slot, rows(3)] = dv[rows(far)].astype(low.dtype)

        c = pltpu.make_async_copy(low.at[slot], message, at(0))
        c.start()
        return [c]

    stores += leave(back_inter, inter_near, inter_far, inter_target, from_inter, 0)
    stores += leave(back_intra, intra_near, intra_far, intra_target, from_intra, 1)
    for c in stores:
        c.wait()


def attend(blocks, piece, width, head_dim, starts, ends, place, q, k, v, g, inter, intra, heads, outs):
    low, high = q.dtype, jnp.float32
    back = jax.ShapeDtypeStruct((2 * SLOTS * BLOCK, width), low)
    whole = jax.ShapeDtypeStruct(q.shape, low)
    total = jax.ShapeDtypeStruct((blocks * BLOCK, width), high)
    sources, targets = (blocks + 2 * SLOTS) * BLOCK, (blocks + 2) * BLOCK
    pairs = blocks * MAX_BAND * (width // (2 * head_dim))
    return pl.pallas_call(
        functools.partial(attend_kernel, blocks, piece, width, head_dim),
        out_shape=(whole, whole, back, back, total, total),
        in_specs=[SMEM] * 3 + [ANY] * (8 + len(outs)),
        out_specs=(ANY,) * 6,
        input_output_aliases={11: 0, 12: 1} if outs else {},
        scratch_shapes=[
            pltpu.VMEM((sources, width), low),
            pltpu.VMEM((sources, width), low),
            pltpu.VMEM((targets, width), low),
            pltpu.VMEM((targets, width), low),
            pltpu.VMEM((sources, width), high),
            pltpu.VMEM((sources, width), high),
            pltpu.VMEM((targets, width), low),
            pltpu.VMEM((targets, width), low),
            pltpu.VMEM((2, 2 * SLOTS * BLOCK, width), low),
            pltpu.VMEM((2, HEADER, width), low),
            pltpu.SemaphoreType.DMA((14,)),
        ],
        compiler_params=pltpu.CompilerParams(vmem_limit_bytes=VMEM_LIMIT),
        cost_estimate=pl.CostEstimate(
            flops=pairs * 12 * BLOCK * 2 * BLOCK * BLOCK, transcendentals=pairs * 2 * BLOCK * BLOCK,
            bytes_accessed=16 * blocks * BLOCK * width,
        ),
        name=f"attend{piece}",
    )(starts, ends, place, q, k, v, g, inter, intra, *heads, *outs)


def settle_kernel(
    blocks, piece, width, starts, ends, place, grad_k, grad_v, inter, intra, *rest
):
    rest = rest[4:] if piece else rest[2:]
    attended, grad_q, out_k, out_v = rest[:4]
    above, below, stage, sem = rest[4:]
    first, odd = place[0], place[1]
    cols = pl.ds(piece * width, width)
    up = moved_up(starts, ends, first, blocks)
    down = moved_down(starts, ends, first)
    is_odd = odd == 1

    @pl.when(is_odd)
    def _():
        run_copies([
            pltpu.make_async_copy(inter, above, sem.at[0]),
            pltpu.make_async_copy(intra, below, sem.at[1]),
        ])

    @pl.when(jnp.logical_not(is_odd))
    def _():
        run_copies([
            pltpu.make_async_copy(intra, above, sem.at[0]),
            pltpu.make_async_copy(inter, below, sem.at[1]),
        ])

    last = blocks - 1
    high = jnp.float32
    keep_up = jnp.logical_not(up)
    keep_down = jnp.logical_not(down)
    for i, (total, stored) in enumerate(((grad_k, stage.at[0]), (grad_v, stage.at[1]))):
        for block in range(blocks):
            value = total[rows(block)]
            if block == 0:
                value += below[rows(i)].astype(high)
            if block == 1:
                far = below[rows(2 + i)].astype(high)
                value += jnp.where(keep_down, far, jnp.zeros_like(far))
            if block == last:
                value += above[rows(i)].astype(high)
            if block == last - 1:
                far = above[rows(2 + i)].astype(high)
                value += jnp.where(keep_up, far, jnp.zeros_like(far))
            stored[rows(block)] = value.astype(stage.dtype)
    stores = [
        pltpu.make_async_copy(stage.at[0], out_k.at[:, cols], sem.at[0]),
        pltpu.make_async_copy(stage.at[1], out_v.at[:, cols], sem.at[1]),
    ]
    for c in stores:
        c.start()

    @pl.when(up)
    def _():
        run_copies([
            pltpu.make_async_copy(above.at[rows(2)], attended.at[rows(last), cols], sem.at[2]),
            pltpu.make_async_copy(above.at[rows(3)], grad_q.at[rows(last), cols], sem.at[3]),
        ])

    @pl.when(down)
    def _():
        run_copies([
            pltpu.make_async_copy(below.at[rows(2)], attended.at[rows(0), cols], sem.at[2]),
            pltpu.make_async_copy(below.at[rows(3)], grad_q.at[rows(0), cols], sem.at[3]),
        ])

    for c in stores:
        c.wait()


def settle(blocks, piece, width, starts, ends, place, grad_k, grad_v, inter, intra, attended, grad_q, outs):
    low = attended.dtype
    whole = jax.ShapeDtypeStruct(attended.shape, low)
    message = 2 * SLOTS * BLOCK
    vmem = pl.BlockSpec(memory_space=pltpu.VMEM)
    aliases = {7: 0, 8: 1}
    if outs:
        aliases.update({9: 2, 10: 3})
    return pl.pallas_call(
        functools.partial(settle_kernel, blocks, piece, width),
        out_shape=(whole,) * 4,
        in_specs=[SMEM] * 3 + [vmem] * 2 + [ANY] * (4 + len(outs)),
        out_specs=(ANY,) * 4,
        input_output_aliases=aliases,
        scratch_shapes=[
            pltpu.VMEM((message, width), low),
            pltpu.VMEM((message, width), low),
            pltpu.VMEM((2, blocks * BLOCK, width), low),
            pltpu.SemaphoreType.DMA((4,)),
        ],
        compiler_params=pltpu.CompilerParams(vmem_limit_bytes=VMEM_LIMIT),
        name=f"settle{piece}",
    )(starts, ends, place, grad_k, grad_v, inter, intra, attended, grad_q, *outs)


def body(q, k, v, g, starts, ends):
    shard_rows, model_width = q.shape
    blocks = shard_rows // BLOCK
    head_dim = model_width // H
    width = model_width // PIECES
    count = lax.axis_size("seq")
    index = lax.axis_index("seq")
    place = jnp.stack([index * blocks, index % 2]).astype(jnp.int32)
    across = [(i, i + 1) for i in range(1, count - 1, 2)] + [(i + 1, i) for i in range(1, count - 1, 2)]
    inside = [(i, i ^ 1) for i in range(count)]
    swap = lambda inter, intra: (lax.ppermute(inter, "seq", across), lax.ppermute(intra, "seq", inside))

    arrived = []
    for piece in range(PIECES):
        arrived.append(swap(*pack(blocks, piece, width, starts, ends, place, q, k, v, g)))
    heads = arrived[0]
    outs, totals, returned = (), [], []
    for piece in range(PIECES):
        results = attend(
            blocks, piece, width, head_dim, starts, ends, place, q, k, v, g, *arrived[piece], heads, outs
        )
        outs = results[:2]
        returned.append(swap(*results[2:4]))
        totals.append(results[4:])
    attended, grad_q = outs
    outs = ()
    for piece in range(PIECES):
        attended, grad_q, *outs = settle(
            blocks, piece, width, starts, ends, place, *totals[piece], *returned[piece], attended, grad_q, outs
        )
    return (attended, grad_q, *outs)


def solution(mesh):
    spec = P(("groups", "seq"), None)
    flat = P(("groups", "seq"))
    return jax.shard_map(
        body,
        mesh=mesh,
        in_specs=(spec, spec, spec, spec, flat, flat),
        out_specs=(spec, spec, spec, spec),
        check_vma=False,
    )
```

time: 301 us -> 136 us (0.45)
  the two profiles are of different devices: /device:TPU:9 before, /device:TPU:6 now
where the time goes in v1:
time: 136 us; the launch traced here: 135 us
  Pallas kernels  112 us (82%)
  starting transfers between devices  11.3 us (8%)
  waiting for transfers between devices  9.93 us (7%)
    pallas_call x2, Pallas kernels, pack(): pl.pallas_call(functools.partial(pack_kernel, blocks, piece, width, heade...  67.3 us
    pallas_call x2, Pallas kernels, attend(): pl.pallas_call(functools.partial(attend_kernel, blocks, piece, width, hea...  40.9 us
    ppermute x4, waiting for transfers between devices, body(): lax.ppermute(inter, 'seq', across)  9.92 us
    ppermute x4, starting transfers between devices, body(): lax.ppermute(inter, 'seq', across)  8.06 us
    pallas_call x2, Pallas kernels, settle(): pl.pallas_call(functools.partial(settle_kernel, blocks, piece, width), ou...  3.78 us
    ppermute x4, starting transfers between devices, body(): lax.ppermute(intra, 'seq', inside)  3.27 us
  transfers between devices with their start and end apart: 8, of which 1 were waited for; matrix products, arithmetic and copies ran while one was open for 0% of the time, Pallas kernels for 57%

profile of v1, /device:TPU:6, one launch (start us, length us, event | category | flops | bytes accessed | tf_op | source)
XLA Modules:
  0.0 134.7 jit_solution(4737593221608455058)
XLA Ops:
  0.6 0.6 pad_add_fusion.place
  1.2 33.6 %pack0.1 = (bf16[528,512]{1,0:T(8,128)(2,1)}, bf16[528,512]{1,0:T(8,128)(2,1)}) custom-call(s32[4]{0:T(128)} %starts.11, s32[4]{0:T(128)} %ends.11, s32[2]{0:T(128)} %pad_add_fusion.place, bf16[512,1024]{1,0:T(8,128)(2,1)} %q.7, bf16[512,1024]{1,0:T(8,128)(2,1)} %k.7, bf16[512,1024]{1,0:T(8,128)(2,1)} %v.7, bf16[512,1024]{1,0:T(8,128)(2,1)} %g.7), custom_call_target="tpu_custom_call" | custom-call | tf_op jit(solution)/shard_map/pack0/pallas_call | solution.py:103
  34.9 1.9 %collective-permute-start.2 = (bf16[528,512]{1,0:T(8,128)(2,1)}, bf16[528,512]{1,0:T(8,128)(2,1)S(1)}, u32[]{:S(2)}, u32[]{:S(2)}) collective-permute-start(bf16[528,512]{1,0:T(8,128)(2,1)} %get-tuple-element.26), channel_id=1, source_target_pairs={{1,2},{3,4},{5,6},{7,8},{9,10},{11,12},{13,14},{2,1},{4,3},{6,5},{... | collective-permute-start | bytes 1622024 | tf_op jit(solution)/shard_map/ppermute | solution.py:430
  36.8 0.0 copy-start
  36.8 1.7 %collective-permute-start.3 = (bf16[528,512]{1,0:T(8,128)(2,1)}, bf16[528,512]{1,0:T(8,128)(2,1)S(1)}, u32[]{:S(2)}, u32[]{:S(2)}) collective-permute-start(bf16[528,512]{1,0:T(8,128)(2,1)} %get-tuple-element.27), channel_id=1, source_target_pairs={{0,1},{1,0},{2,3},{3,2},{4,5},{5,4},{6,7},{7,6},{8,9},{9,8},{10,11... | collective-permute-start | bytes 1622024 | tf_op jit(solution)/shard_map/ppermute | solution.py:430
  38.5 33.6 %pack1.1 = (bf16[512,512]{1,0:T(8,128)(2,1)}, bf16[512,512]{1,0:T(8,128)(2,1)}) custom-call(s32[4]{0:T(128)} %starts.11, s32[4]{0:T(128)} %ends.11, s32[2]{0:T(128)} %pad_add_fusion.place, bf16[512,1024]{1,0:T(8,128)(2,1)} %q.7, bf16[512,1024]{1,0:T(8,128)(2,1)} %k.7, bf16[512,1024]{1,0:T(8,128)(2,1)} %v.7, bf16[512,1024]{1,0:T(8,128)(2,1)} %g.7), custom_call_target="tpu_custom_call" | custom-call | tf_op jit(solution)/shard_map/pack1/pallas_call | solution.py:103
  72.2 0.0 copy-start.1
  72.2 0.0 copy-start.2
  72.2 0.0 copy-start.3
  72.2 2.3 %collective-permute-start = (bf16[512,512]{1,0:T(8,128)(2,1)}, bf16[512,512]{1,0:T(8,128)(2,1)S(1)}, u32[]{:S(2)}, u32[]{:S(2)}) collective-permute-start(bf16[512,512]{1,0:T(8,128)(2,1)} %get-tuple-element.24), channel_id=1, source_target_pairs={{1,2},{3,4},{5,6},{7,8},{9,10},{11,12},{13,14},{2,1},{4,3},{6,5},{... | collective-permute-start | bytes 1572872 | tf_op jit(solution)/shard_map/ppermute | solution.py:430
  74.5 1.4 %collective-permute-start.1 = (bf16[512,512]{1,0:T(8,128)(2,1)}, bf16[512,512]{1,0:T(8,128)(2,1)S(1)}, u32[]{:S(2)}, u32[]{:S(2)}) collective-permute-start(bf16[512,512]{1,0:T(8,128)(2,1)} %get-tuple-element.25), channel_id=1, source_target_pairs={{0,1},{1,0},{2,3},{3,2},{4,5},{5,4},{6,7},{7,6},{8,9},{9,8},{10,11... | collective-permute-start | bytes 1572872 | tf_op jit(solution)/shard_map/ppermute | solution.py:430
  75.9 0.0 collective-permute-done.2.inter.inter_head
  75.9 0.0 collective-permute-done.3.intra.intra_head
  75.9 0.0 copy-done
  76.0 0.0 copy-done.1
  76.0 0.0 copy-done.2
  76.0 0.0 copy-done.3
  76.0 20.5 %attend0.1 = (bf16[512,1024]{1,0:T(8,128)(2,1)}, bf16[512,1024]{1,0:T(8,128)(2,1)}, bf16[512,512]{1,0:T(8,128)(2,1)S(1)}, bf16[512,512]{1,0:T(8,128)(2,1)S(1)}, ...) custom-call(s32[4]{0:T(128)S(1)} %copy-done.1, s32[4]{0:T(128)S(1)} %copy-done.2, s32[2]{0:T(128)S(1)} %copy-done.3, ...), custom_call_target="tpu_custom_call" | custom-call | flops 3221225472 | bytes 4194304 | tf_op jit(solution)/shard_map/attend0/pallas_call | solution.py:298
  96.5 1.9 %collective-permute-start.6 = (bf16[512,512]{1,0:T(8,128)(2,1)S(1)}, bf16[512,512]{1,0:T(8,128)(2,1)S(1)}, u32[]{:S(2)}, u32[]{:S(2)}) collective-permute-start(bf16[512,512]{1,0:T(8,128)(2,1)S(1)} %get-tuple-element.36), channel_id=1, source_target_pairs={{1,2},{3,4},{5,6},{7,8},{9,10},{11,12},{13,14},{2,1},{4,3},{6,5},{... | collective-permute-start | bytes 1572872 | tf_op jit(solution)/shard_map/ppermute | solution.py:430
  98.4 0.1 collective-permute-start.7
  98.5 0.0 collective-permute-done.inter
  98.5 0.0 collective-permute-done.1.intra
  98.5 20.4 %attend1.1 = (bf16[512,1024]{1,0:T(8,128)(2,1)}, bf16[512,1024]{1,0:T(8,128)(2,1)}, bf16[512,512]{1,0:T(8,128)(2,1)S(1)}, bf16[512,512]{1,0:T(8,128)(2,1)S(1)}, ...) custom-call(s32[4]{0:T(128)S(1)} %copy-done.1, s32[4]{0:T(128)S(1)} %copy-done.2, ...), custom_call_target="tpu_custom_call", output_to_operand_aliasing={{0}: (11, {}), {1}: (12, {})} | custom-call | flops 3221225472 | bytes 4194304 | tf_op jit(solution)/shard_map/attend1/pallas_call | solution.py:298
  118.9 1.9 %collective-permute-start.4 = (bf16[512,512]{1,0:T(8,128)(2,1)S(1)}, bf16[512,512]{1,0:T(8,128)(2,1)S(1)}, u32[]{:S(2)}, u32[]{:S(2)}) collective-permute-start(bf16[512,512]{1,0:T(8,128)(2,1)S(1)} %get-tuple-element.32), channel_id=1, source_target_pairs={{1,2},{3,4},{5,6},{7,8},{9,10},{11,12},{13,14},{2,1},{4,3},{6,5},{... | collective-permute-start | bytes 1572872 | tf_op jit(solution)/shard_map/ppermute | solution.py:430
  120.9 0.1 collective-permute-start.5
  120.9 0.0 collective-permute-done.6.inter
  121.0 0.0 collective-permute-done.7.intra
  121.0 1.9 %settle0.1 = (bf16[512,1024]{1,0:T(8,128)(2,1)}, bf16[512,1024]{1,0:T(8,128)(2,1)}, bf16[512,1024]{1,0:T(8,128)(2,1)}, bf16[512,1024]{1,0:T(8,128)(2,1)}) custom-call(s32[4]{0:T(128)S(1)} %copy-done.1, s32[4]{0:T(128)S(1)} %copy-done.2, s32[2]{0:T(128)S(1)} %copy-done.3, ...), custom_call_target="tpu_custom_call", output_to_operand_aliasing={{0}: (7, {}), {1}: (8, {})} | custom-call | tf_op jit(solution)/shard_map/settle0/pallas_call | solution.py:403
  122.9 9.9 %collective-permute-done.4.inter = bf16[512,512]{1,0:T(8,128)(2,1)S(1)} collective-permute-done((bf16[512,512]{1,0:T(8,128)(2,1)S(1)}, bf16[512,512]{1,0:T(8,128)(2,1)S(1)}, u32[]{:S(2)}, u32[]{:S(2)}) %collective-permute-start.4) | collective-permute-done | bytes 524320 | tf_op jit(solution)/shard_map/ppermute | solution.py:430
  132.8 0.0 collective-permute-done.5.intra
  132.8 1.9 %settle1.1 = (bf16[512,1024]{1,0:T(8,128)(2,1)}, bf16[512,1024]{1,0:T(8,128)(2,1)}, bf16[512,1024]{1,0:T(8,128)(2,1)}, bf16[512,1024]{1,0:T(8,128)(2,1)}) custom-call(s32[4]{0:T(128)S(1)} %copy-done.1, s32[4]{0:T(128)S(1)} %copy-done.2, s32[2]{0:T(128)S(1)} %copy-done.3, ...), custom_call_target="tpu_custom_call", output_to_operand_aliasing={{0}: (7, {}), {1}: (8, {}), {2}: (9, {}), {3}: (10, {})} | custom-call | tf_op jit(solution)/shard_map/settle1/pallas_call | solution.py:403
Async XLA Ops:
  34.9 41.1 %collective-permute-start.2 = (bf16[528,512]{1,0:T(8,128)(2,1)}, bf16[528,512]{1,0:T(8,128)(2,1)S(1)}, u32[]{:S(2)}, u32[]{:S(2)}) collective-permute-start(bf16[528,512]{1,0:T(8,128)(2,1)} %get-tuple-element.26), channel_id=1, source_target_pairs={{1,2},{3,4},{5,6},{7,8},{9,10},{11,12},{13,14},{2,1},{4,3},{6,5},{... | collective-permute-start | bytes 1622024 | tf_op jit(solution)/shard_map/ppermute | solution.py:430
  36.8 39.1 %copy-start = (bf16[512,1024]{1,0:T(8,128)(2,1)S(1)}, bf16[512,1024]{1,0:T(8,128)(2,1)}, u32[]{:S(2)}) copy-start(bf16[512,1024]{1,0:T(8,128)(2,1)} %q.7) | copy-start | bytes 3145732
  36.8 39.1 %collective-permute-start.3 = (bf16[528,512]{1,0:T(8,128)(2,1)}, bf16[528,512]{1,0:T(8,128)(2,1)S(1)}, u32[]{:S(2)}, u32[]{:S(2)}) collective-permute-start(bf16[528,512]{1,0:T(8,128)(2,1)} %get-tuple-element.27), channel_id=1, source_target_pairs={{0,1},{1,0},{2,3},{3,2},{4,5},{5,4},{6,7},{7,6},{8,9},{9,8},{10,11... | collective-permute-start | bytes 1622024 | tf_op jit(solution)/shard_map/ppermute | solution.py:430
  72.2 3.8 %copy-start.1 = (s32[4]{0:T(128)S(1)}, s32[4]{0:T(128)}, u32[]{:S(2)}) copy-start(s32[4]{0:T(128)} %starts.11) | copy-start | bytes 52
  72.2 3.8 %copy-start.2 = (s32[4]{0:T(128)S(1)}, s32[4]{0:T(128)}, u32[]{:S(2)}) copy-start(s32[4]{0:T(128)} %ends.11) | copy-start | bytes 52
  72.2 3.8 %copy-start.3 = (s32[2]{0:T(128)S(1)}, s32[2]{0:T(128)}, u32[]{:S(2)}) copy-start(s32[2]{0:T(128)} %pad_add_fusion.place) | copy-start | bytes 28
  72.2 26.3 %collective-permute-start = (bf16[512,512]{1,0:T(8,128)(2,1)}, bf16[512,512]{1,0:T(8,128)(2,1)S(1)}, u32[]{:S(2)}, u32[]{:S(2)}) collective-permute-start(bf16[512,512]{1,0:T(8,128)(2,1)} %get-tuple-element.24), channel_id=1, source_target_pairs={{1,2},{3,4},{5,6},{7,8},{9,10},{11,12},{13,14},{2,1},{4,3},{6,5},{... | collective-permute-start | bytes 1572872 | tf_op jit(solution)/shard_map/ppermute | solution.py:430
  74.5 24.0 %collective-permute-start.1 = (bf16[512,512]{1,0:T(8,128)(2,1)}, bf16[512,512]{1,0:T(8,128)(2,1)S(1)}, u32[]{:S(2)}, u32[]{:S(2)}) collective-permute-start(bf16[512,512]{1,0:T(8,128)(2,1)} %get-tuple-element.25), channel_id=1, source_target_pairs={{0,1},{1,0},{2,3},{3,2},{4,5},{5,4},{6,7},{7,6},{8,9},{9,8},{10,11... | collective-permute-start | bytes 1572872 | tf_op jit(solution)/shard_map/ppermute | solution.py:430
  96.5 24.5 %collective-permute-start.6 = (bf16[512,512]{1,0:T(8,128)(2,1)S(1)}, bf16[512,512]{1,0:T(8,128)(2,1)S(1)}, u32[]{:S(2)}, u32[]{:S(2)}) collective-permute-start(bf16[512,512]{1,0:T(8,128)(2,1)S(1)} %get-tuple-element.36), channel_id=1, source_target_pairs={{1,2},{3,4},{5,6},{7,8},{9,10},{11,12},{13,14},{2,1},{4,3},{6,5},{... | collective-permute-start | bytes 1572872 | tf_op jit(solution)/shard_map/ppermute | solution.py:430
  98.4 22.6 %collective-permute-start.7 = (bf16[512,512]{1,0:T(8,128)(2,1)S(1)}, bf16[512,512]{1,0:T(8,128)(2,1)S(1)}, u32[]{:S(2)}, u32[]{:S(2)}) collective-permute-start(bf16[512,512]{1,0:T(8,128)(2,1)S(1)} %get-tuple-element.37), channel_id=1, source_target_pairs={{0,1},{1,0},{2,3},{3,2},{4,5},{5,4},{6,7},{7,6},{8,9},{9,8},{10,11... | collective-permute-start | bytes 1572872 | tf_op jit(solution)/shard_map/ppermute | solution.py:430
  118.9 13.8 %collective-permute-start.4 = (bf16[512,512]{1,0:T(8,128)(2,1)S(1)}, bf16[512,512]{1,0:T(8,128)(2,1)S(1)}, u32[]{:S(2)}, u32[]{:S(2)}) collective-permute-start(bf16[512,512]{1,0:T(8,128)(2,1)S(1)} %get-tuple-element.32), channel_id=1, source_target_pairs={{1,2},{3,4},{5,6},{7,8},{9,10},{11,12},{13,14},{2,1},{4,3},{6,5},{... | collective-permute-start | bytes 1572872 | tf_op jit(solution)/shard_map/ppermute | solution.py:430
  120.9 11.9 %collective-permute-start.5 = (bf16[512,512]{1,0:T(8,128)(2,1)S(1)}, bf16[512,512]{1,0:T(8,128)(2,1)S(1)}, u32[]{:S(2)}, u32[]{:S(2)}) collective-permute-start(bf16[512,512]{1,0:T(8,128)(2,1)S(1)} %get-tuple-element.33), channel_id=1, source_target_pairs={{0,1},{1,0},{2,3},{3,2},{4,5},{5,4},{6,7},{7,6},{8,9},{9,8},{10,11... | collective-permute-start | bytes 1572872 | tf_op jit(solution)/shard_map/ppermute | solution.py:430
